TPU v7x, 128 devices: a whole 4x4x4 slice. The times are simulated.
128 devices in a mesh: snap: 4 (over z_lo, core), pts: 32 (over z_hi, x, y).
Axes of the slice: x: 4, y: 4, z: 4 (z_hi: 2, z_lo: 2; z = z_hi * 2 + z_lo), core: 2. Of those that a mesh axis runs over, the one named last changes fastest.
Arguments:
- strains: bfloat16 [6, 512, 131072], P(None, 'snap', 'pts'), may hold values from -3 to 3
- moduli: float32 [2, 131072], P(None, 'pts'), may hold values from 0.5 to 2
- range_test: bfloat16 [131072, 256], P('pts'), may hold values from -0.015625 to 0.015625
- corange_test: bfloat16 [256, 512], replicated, may hold values from -0.25 to 0.25
- core_left: float32 [512, 512], P(None, 'snap'), may hold values from -0.25 to 0.25
- core_right: bfloat16 [512, 131072], P(None, 'pts'), may hold values from -0.015625 to 0.015625
Outputs:
- range_sketch: float32 [512, 256], P('snap')
- corange_sketch: float32 [256, 131072], P('snap', 'pts')
- core_sketch: float32 [512, 512], replicated
All inputs are finite; a program needn't handle non-finite values.
Results may differ from a plain program's by a relative error of at most 0.0031.
Values may be sent and summed in bfloat16 or wider, within the bound.
A program may use at most 64 MiB of HBM per device.

v0:
```python
import math
import jax
import jax.numpy as jnp
from jax import lax
from jax.sharding import PartitionSpec as P


def energy_field(strains, moduli):
    strain_xx = strains[0].astype(jnp.float32)
    strain_yy = strains[1].astype(jnp.float32)
    strain_zz = strains[2].astype(jnp.float32)
    strain_xy = strains[3].astype(jnp.float32)
    strain_yz = strains[4].astype(jnp.float32)
    strain_xz = strains[5].astype(jnp.float32)
    lame_first = moduli[0][None, :]
    shear_mod = moduli[1][None, :]
    strain_trace = strain_xx + strain_yy + strain_zz
    mean_strain = strain_trace / 3.0
    dev_xx = strain_xx - mean_strain
    dev_yy = strain_yy - mean_strain
    dev_zz = strain_zz - mean_strain
    dev_square = (
        dev_xx * dev_xx
        + dev_yy * dev_yy
        + dev_zz * dev_zz
        + 2.0 * (strain_xy * strain_xy + strain_yz * strain_yz + strain_xz * strain_xz)
    ) / 6.0
    dev_norm = jnp.sqrt(dev_square)
    dev_det = (
        dev_xx * (dev_yy * dev_zz - strain_yz * strain_yz)
        - strain_xy * (strain_xy * dev_zz - strain_yz * strain_xz)
        + strain_xz * (strain_xy * strain_yz - dev_yy * strain_xz)
    )
    sine_part = jnp.sqrt(
        jnp.maximum(4.0 * dev_square * dev_square * dev_square - dev_det * dev_det, 0.0)
    )
    angle_third = jnp.arctan2(sine_part, dev_det) / 3.0
    positive_trace = jnp.maximum(strain_trace, 0.0)
    density = 0.5 * lame_first * positive_trace * positive_trace
    for order in range(3):
        principal = mean_strain + 2.0 * dev_norm * jnp.cos(
            angle_third - 2.0 * math.pi * order / 3.0
        )
        positive = jnp.maximum(principal, 0.0)
        density = density + shear_mod * positive * positive
    return density.astype(jnp.bfloat16)


def per_device(strains, moduli, range_test, corange_test, core_left, core_right):
    energy = energy_field(strains, moduli)
    snap_rows = energy.shape[0]
    range_part = jnp.dot(energy, range_test, preferred_element_type=jnp.float32)
    cross_part = lax.dot_general(
        energy, core_right, (((1,), (1,)), ((), ())), preferred_element_type=jnp.float32
    )
    range_sketch = lax.psum(range_part, "pts")
    core_share = jnp.dot(core_left, cross_part, precision=lax.Precision.HIGHEST)
    core_sketch = lax.psum(core_share, ("snap", "pts"))
    own_cols = lax.dynamic_slice_in_dim(
        corange_test, lax.axis_index("snap") * snap_rows, snap_rows, 1
    )
    corange_sketch = lax.psum_scatter(
        jnp.dot(own_cols, energy, preferred_element_type=jnp.float32),
        "snap",
        scatter_dimension=0,
        tiled=True,
    )
    return (range_sketch, corange_sketch, core_sketch)


def solution(mesh):
    in_specs = (
        P(None, "snap", "pts"),
        P(None, "pts"),
        P("pts", None),
        P(),
        P(None, "snap"),
        P(None, "pts"),
    )
    out_specs = (P("snap", None), P("snap", "pts"), P())
    return jax.shard_map(
        per_device, mesh=mesh, in_specs=in_specs, out_specs=out_specs, check_vma=False
    )
```

profile of v0, /device:TPU:0, one launch (start us, length us, event | category | flops | bytes accessed | tf_op | source)
XLA Modules:
  0.0 557.0 jit_solution(8219614878723953401)
XLA Ops:
  8.0 0.0 copy-start
  8.0 0.0 all-reduce.5.cloned.1.call-start
  8.1 0.9 slice_multiply_fusion
  9.0 0.0 copy-start.1
  9.0 31.8 %fusion.11 = bf16[128,4096]{1,0:T(8,128)(2,1)S(1)} fusion(bf16[6,128,4096]{2,1,0:T(8,128)(2,1)} %param.6, f32[4096]{0:T(1024)S(1)} %bitcast.30, f32[4096]{0:T(1024)S(1)} %bitcast.29), kind=kLoop, calls=%fused_computation.30 | loop fusion | flops 36700160 | bytes 7372800 | tf_op jit(solution)/shard_map/convert_element_type | solution.py:46
  40.9 0.0 copy-done.1
  40.9 0.0 copy-start.2
  40.9 1.5 fusion.27
  42.4 0.0 copy-done.2
  42.4 2.0 convolution_bitcast_fusion
  44.4 0.0 all-reduce.5.cloned.1.call-update
  44.5 0.0 all-reduce.3.cloned.1.call-start
  44.5 0.0 copy-done
  44.5 1.1 fusion.26
  45.6 0.0 all-reduce.3.cloned.1.call-update
  45.7 0.0 reduce-scatter.2.cloned.1.call-start
  45.7 3.5 fusion.23
  49.2 0.0 reduce-scatter.2.cloned.1.call-update
  49.2 170.6 %all-reduce.5.cloned.1.call-done = f32[512,512]{0,1:T(8,128)} async-done(((f32[512,512]{0,1:T(8,128)}), f32[512,512]{0,1:T(8,128)}) %all-reduce.5.cloned.1.call-update) | async-done | bytes 1048592 | tf_op jit(solution)/shard_map/psum | solution.py:58
  219.8 2.5 copy.9
  222.3 325.7 %all-reduce.3.cloned.1.call-done = f32[128,256]{1,0:T(8,128)} async-done(((f32[128,256]{1,0:T(8,128)}), f32[128,256]{1,0:T(8,128)}) %all-reduce.3.cloned.1.call-update) | async-done | bytes 131088 | tf_op jit(solution)/shard_map/psum | solution.py:56
  548.0 0.0 reduce-scatter.2.cloned.1.call-done
  548.0 1.6 copy.12
Async XLA Ops:
  8.0 36.5 %copy-start = (bf16[4096,256]{1,0:T(8,128)(2,1)S(1)}, bf16[4096,256]{1,0:T(8,128)(2,1)}, u32[]{:S(2)}) copy-start(bf16[4096,256]{1,0:T(8,128)(2,1)} %param.8) | copy-start | bytes 6291460
  8.0 211.8 %all-reduce.5.cloned.1.call-start = ((), (), s32[]{:S(2)}) async-start(), calls=%async_computation.3 | async-start | bytes 2097152 | tf_op jit(solution)/shard_map/psum | solution.py:58
  9.0 31.9 %copy-start.1 = (bf16[512,4096]{1,0:T(8,128)(2,1)S(1)}, bf16[512,4096]{1,0:T(8,128)(2,1)}, u32[]{:S(2)}) copy-start(bf16[512,4096]{1,0:T(8,128)(2,1)} %param.11) | copy-start | bytes 12582916
  40.9 1.6 copy-start.2
  44.5 503.6 %all-reduce.3.cloned.1.call-start = ((), (), s32[]{:S(2)}) async-start(), calls=%async_computation.1 | async-start | bytes 262144 | tf_op jit(solution)/shard_map/psum | solution.py:56
  45.7 502.4 %reduce-scatter.2.cloned.1.call-start = ((), (), s32[]{:S(2)}) async-start(), calls=%async_computation.2 | async-start | bytes 5242880 | tf_op jit(solution)/shard_map/reduce_scatter | solution.py:62
Sparse Core Ops, SparseCore 0:
  44.6 175.1 all-reduce.4
  222.8 325.1 all-reduce.2
Sparse Core Ops, SparseCore 1:
  49.3 47.8 reduce-scatter.1
where the time goes:
time: 557 us
  waiting for transfers between devices  496 us (89%)
  other arithmetic  32.8 us (6%)
  between operations  15.6 us (3%)
  matrix products  8.11 us (1%)
    psum x1, waiting for transfers between devices, per_device(): range_sketch = lax.psum(range_part, 'pts')  326 us
    psum x1, waiting for transfers between devices, per_device(): core_sketch = lax.psum(core_share, ('snap', 'pts'))  171 us
    convert_element_type x1, other arithmetic, energy_field(): return density.astype(jnp.bfloat16)  31.8 us
  transfers between devices with their start and end apart: 3, of which 2 were waited for; matrix products, arithmetic and copies ran while one was open for 1% of the time, Pallas kernels for 0%

commit v1 on v0

--- a/solution.py
+++ b/solution.py
@@ -55,7 +55,7 @@
     )
     range_sketch = lax.psum(range_part, "pts")
     core_share = jnp.dot(core_left, cross_part, precision=lax.Precision.HIGHEST)
-    core_sketch = lax.psum(core_share, ("snap", "pts"))
+    core_sketch = lax.psum(lax.psum(core_share, "snap"), "pts")
     own_cols = lax.dynamic_slice_in_dim(
         corange_test, lax.axis_index("snap") * snap_rows, snap_rows, 1
     )

time: 557 us -> 497 us (0.89)
  waiting for transfers between devices: 496 us -> 438 us
    psum x1, waiting for transfers between devices: 171 us -> 42.7 us  [per_device(): core_sketch = lax.psum(lax.psum(core_share, 'snap'), 'pts')]
    reduce_scatter x1, waiting for transfers between devices: 0.01 us -> 44.4 us  [per_device(): lax.psum_scatter(jnp.dot(own_cols, energy, preferred_element_type=jnp.flo...]
    psum x1, waiting for transfers between devices: 326 us -> 351 us  [per_device(): range_sketch = lax.psum(range_part, 'pts')]
  transfers between devices with their start and end apart: 3 -> 3, of which waited for: 2 -> 3; matrix products, arithmetic and copies ran while one was open for 1% -> 1% of each run, Pallas kernels for 0% -> 0%
where the time goes in v1:
time: 497 us; the launch traced here: 496 us
  waiting for transfers between devices  438 us (88%)
  other arithmetic  32.8 us (7%)
  between operations  13.8 us (3%)
  matrix products  8.11 us (2%)
    psum x1, waiting for transfers between devices, per_device(): range_sketch = lax.psum(range_part, 'pts')  351 us
    reduce_scatter x1, waiting for transfers between devices, per_device(): lax.psum_scatter(jnp.dot(own_cols, energy, preferred_element_type=jnp.flo...  44.4 us
    psum x1, waiting for transfers between devices, per_device(): core_sketch = lax.psum(lax.psum(core_share, 'snap'), 'pts')  42.7 us
    convert_element_type x1, other arithmetic, energy_field(): return density.astype(jnp.bfloat16)  31.8 us
  transfers between devices with their start and end apart: 3, of which 3 were waited for; matrix products, arithmetic and copies ran while one was open for 1% of the time, Pallas kernels for 0%

profile of v1, /device:TPU:0, one launch (start us, length us, event | category | flops | bytes accessed | tf_op | source)
XLA Modules:
  0.0 495.8 jit_solution(6863971252179138947)
XLA Ops:
  7.2 0.0 copy-start
  7.2 0.0 all-reduce.4.cloned.1.call-start
  7.2 0.9 slice_multiply_fusion
  8.2 0.0 copy-start.1
  8.2 31.8 %fusion.11 = bf16[128,4096]{1,0:T(8,128)(2,1)S(1)} fusion(bf16[6,128,4096]{2,1,0:T(8,128)(2,1)} %param.6, f32[4096]{0:T(1024)S(1)} %bitcast.30, f32[4096]{0:T(1024)S(1)} %bitcast.29), kind=kLoop, calls=%fused_computation.30 | loop fusion | flops 36700160 | bytes 7372800 | tf_op jit(solution)/shard_map/convert_element_type | solution.py:46
  40.0 0.0 copy-done.1
  40.1 0.0 copy-start.2
  40.1 1.5 fusion.27
  41.6 0.0 copy-done.2
  41.6 2.0 convolution_bitcast_fusion
  43.6 0.0 all-reduce.4.cloned.1.call-update
  43.6 0.0 all-reduce.6.cloned.1.call-start
  43.7 0.0 copy-done
  43.7 1.1 fusion.26
  44.8 42.7 %all-reduce.4.cloned.1.call-done = f32[512,512]{0,1:T(8,128)} async-done(((f32[512,512]{0,1:T(8,128)}), f32[512,512]{0,1:T(8,128)}) %all-reduce.4.cloned.1.call-update) | async-done | bytes 1048592 | tf_op jit(solution)/shard_map/psum | solution.py:58
  87.5 0.0 all-reduce.6.cloned.1.call-update
  87.6 0.0 reduce-scatter.2.cloned.1.call-start
  87.6 3.5 fusion.23
  91.1 0.0 reduce-scatter.2.cloned.1.call-update
  91.1 350.5 %all-reduce.6.cloned.1.call-done = (f32[128,256]{1,0:T(8,128)}, f32[512,512]{0,1:T(8,128)}) async-done(((f32[128,256]{1,0:T(8,128)}, f32[512,512]{0,1:T(8,128)}), (f32[128,256]{1,0:T(8,128)}, f32[512,512]{0,1:T(8,128)})) %all-reduce.6.cloned.1.call-update) | async-done | bytes 1179664 | tf_op jit(solution)/shard_map/psum | solution.py:56
  441.7 0.0 copy-start.3
  441.7 2.6 copy.9
  444.2 44.4 %reduce-scatter.2.cloned.1.call-done = f32[64,4096]{1,0:T(8,128)} async-done(((f32[256,4096]{1,0:T(8,128)}), f32[64,4096]{1,0:T(8,128)}) %reduce-scatter.2.cloned.1.call-update) | async-done | bytes 1048592 | tf_op jit(solution)/shard_map/reduce_scatter | solution.py:62
  488.6 0.0 copy-done.3
  488.6 0.7 copy.13
Async XLA Ops:
  7.2 36.5 %copy-start = (bf16[4096,256]{1,0:T(8,128)(2,1)S(1)}, bf16[4096,256]{1,0:T(8,128)(2,1)}, u32[]{:S(2)}) copy-start(bf16[4096,256]{1,0:T(8,128)(2,1)} %param.8) | copy-start | bytes 6291460
  7.2 80.4 %all-reduce.4.cloned.1.call-start = ((), (), s32[]{:S(2)}) async-start(), calls=%async_computation.2 | async-start | bytes 2097152 | tf_op jit(solution)/shard_map/psum | solution.py:58
  8.2 31.9 %copy-start.1 = (bf16[512,4096]{1,0:T(8,128)(2,1)S(1)}, bf16[512,4096]{1,0:T(8,128)(2,1)}, u32[]{:S(2)}) copy-start(bf16[512,4096]{1,0:T(8,128)(2,1)} %param.11) | copy-start | bytes 12582916
  40.1 1.6 copy-start.2
  43.6 398.0 %all-reduce.6.cloned.1.call-start = ((), (), s32[]{:S(2)}) async-start(), calls=%async_computation.3 | async-start | bytes 2359296 | tf_op jit(solution)/shard_map/psum | solution.py:56
  87.6 401.1 %reduce-scatter.2.cloned.1.call-start = ((), (), s32[]{:S(2)}) async-start(), calls=%async_computation.1 | async-start | bytes 5242880 | tf_op jit(solution)/shard_map/reduce_scatter | solution.py:62
  441.7 47.0 %copy-start.3 = (f32[128,256]{1,0:T(8,128)S(1)}, f32[128,256]{1,0:T(8,128)}, u32[]{:S(2)}) copy-start(f32[128,256]{1,0:T(8,128)} %get-tuple-element.10) | copy-start | bytes 393220
Sparse Core Ops, SparseCore 0:
  43.8 43.7 all-reduce.3
  90.7 350.9 all-reduce.5
  444.6 43.9 reduce-scatter.1

commit v2 on v0

--- a/solution.py
+++ b/solution.py
@@ -53,7 +53,7 @@
     cross_part = lax.dot_general(
         energy, core_right, (((1,), (1,)), ((), ())), preferred_element_type=jnp.float32
     )
-    range_sketch = lax.psum(range_part, "pts")
+    range_sketch = jnp.sum(lax.all_gather(range_part, "pts"), axis=0)
     core_share = jnp.dot(core_left, cross_part, precision=lax.Precision.HIGHEST)
     core_sketch = lax.psum(core_share, ("snap", "pts"))
     own_cols = lax.dynamic_slice_in_dim(

time: 557 us -> 266 us (0.48)
  waiting for transfers between devices: 496 us -> 202 us
    psum x1 -> x0, waiting for transfers between devices: 326 us -> none  [per_device(): range_sketch = lax.psum(range_part, 'pts')]
    reduce_scatter x1, waiting for transfers between devices: 0.01 us -> 42 us  [per_device(): lax.psum_scatter(jnp.dot(own_cols, energy, preferred_element_type=jnp.flo...]
    psum x1, waiting for transfers between devices: 171 us -> 160 us  [per_device(): core_sketch = lax.psum(core_share, ('snap', 'pts'))]
  transfers between devices with their start and end apart: 3 -> 3, of which waited for: 2 -> 2; matrix products, arithmetic and copies ran while one was open for 1% -> 4% of each run, Pallas kernels for 0% -> 0%
where the time goes in v2:
time: 266 us; the launch traced here: 264 us
  waiting for transfers between devices  202 us (76%)
  other arithmetic  35.9 us (13%)
  between operations  15.6 us (6%)
  matrix products  8.14 us (3%)
    psum x1, waiting for transfers between devices, per_device(): core_sketch = lax.psum(core_share, ('snap', 'pts'))  160 us
    reduce_scatter x1, waiting for transfers between devices, per_device(): lax.psum_scatter(jnp.dot(own_cols, energy, preferred_element_type=jnp.flo...  42 us
    convert_element_type x1, other arithmetic, energy_field(): return density.astype(jnp.bfloat16)  31.8 us
  transfers between devices with their start and end apart: 3, of which 2 were waited for; matrix products, arithmetic and copies ran while one was open for 4% of the time, Pallas kernels for 0%

profile of v2, /device:TPU:0, one launch (start us, length us, event | category | flops | bytes accessed | tf_op | source)
XLA Modules:
  0.0 264.3 jit_solution(1925088228369590594)
XLA Ops:
  8.0 0.0 copy-start
  8.0 0.0 all-reduce.2.cloned.1.call-start
  8.1 0.9 slice_multiply_fusion
  9.0 0.0 copy-start.1
  9.0 31.8 %fusion.11 = bf16[128,4096]{1,0:T(8,128)(2,1)S(1)} fusion(bf16[6,128,4096]{2,1,0:T(8,128)(2,1)} %param.6, f32[4096]{0:T(1024)S(1)} %bitcast.32, f32[4096]{0:T(1024)S(1)} %bitcast.31), kind=kLoop, calls=%fused_computation.30 | loop fusion | flops 36700160 | bytes 7372800 | tf_op jit(solution)/shard_map/convert_element_type | solution.py:46
  40.9 0.0 copy-done.1
  40.9 0.0 copy-start.2
  40.9 1.5 fusion.27
  42.4 0.0 copy-done.2
  42.4 2.0 convolution_bitcast_fusion
  44.4 0.0 all-reduce.2.cloned.1.call-update
  44.5 0.0 all-gather.3.cloned.1.call-start
  44.5 0.0 copy-done
  44.5 1.1 fusion.26
  45.6 0.0 all-gather.3.cloned.1.call-update
  45.7 0.0 reduce-scatter.2.cloned.1.call-start
  45.7 3.5 %fusion.23 = f32[256,4096]{1,0:T(8,128)} fusion(bf16[128,4096]{1,0:T(8,128)(2,1)S(1)} %fusion.11, bf16[256,512]{1,0:T(8,128)(2,1)} %param.9, s32[]{:T(128)S(6)} %select_n.3), kind=kOutput, calls=%fused_computation.43 | convolution fusion | flops 268435456 | bytes 5308420 | tf_op jit(solution)/shard_map/dot_general | solution.py:63
  49.2 0.0 reduce-scatter.2.cloned.1.call-update
  49.2 160.0 %all-reduce.2.cloned.1.call-done = f32[512,512]{0,1:T(8,128)} async-done(((f32[512,512]{0,1:T(8,128)}), f32[512,512]{0,1:T(8,128)}) %all-reduce.2.cloned.1.call-update) | async-done | bytes 1048592 | tf_op jit(solution)/shard_map/psum | solution.py:58
  209.3 2.5 copy.9
  211.8 0.0 all-gather.3.cloned.1.call-done
  211.8 3.1 %reduce_sum.9 = f32[128,256]{1,0:T(8,128)} reduce(f32[32,128,256]{2,1,0:T(8,128)} %bitcast.30, f32[]{:T(128)} %constant.8.clone.1), dimensions={0}, to_apply=%region_0.0 | reduce | flops 1015808 | bytes 4325380 | tf_op jit(solution)/shard_map/reduce_sum | solution.py:56
  214.9 42.0 %reduce-scatter.2.cloned.1.call-done = f32[64,4096]{1,0:T(8,128)} async-done(((f32[256,4096]{1,0:T(8,128)}), f32[64,4096]{1,0:T(8,128)}) %reduce-scatter.2.cloned.1.call-update) | async-done | bytes 1048592 | tf_op jit(solution)/shard_map/reduce_scatter | solution.py:62
Async XLA Ops:
  8.0 36.5 %copy-start = (bf16[4096,256]{1,0:T(8,128)(2,1)S(1)}, bf16[4096,256]{1,0:T(8,128)(2,1)}, u32[]{:S(2)}) copy-start(bf16[4096,256]{1,0:T(8,128)(2,1)} %param.8) | copy-start | bytes 6291460
  8.0 201.3 %all-reduce.2.cloned.1.call-start = ((), (), s32[]{:S(2)}) async-start(), calls=%async_computation.2 | async-start | bytes 2097152 | tf_op jit(solution)/shard_map/psum | solution.py:58
  9.0 31.9 %copy-start.1 = (bf16[512,4096]{1,0:T(8,128)(2,1)S(1)}, bf16[512,4096]{1,0:T(8,128)(2,1)}, u32[]{:S(2)}) copy-start(bf16[512,4096]{1,0:T(8,128)(2,1)} %param.11) | copy-start | bytes 12582916
  40.9 1.6 copy-start.2
  44.5 167.3 %all-gather.3.cloned.1.call-start = ((), (), s32[]{:S(2)}) async-start(), calls=%async_computation.3 | async-start | bytes 4325376 | tf_op jit(solution)/shard_map/all_gather | solution.py:56
  45.7 211.2 %reduce-scatter.2.cloned.1.call-start = ((), (), s32[]{:S(2)}) async-start(), calls=%async_computation.1 | async-start | bytes 5242880 | tf_op jit(solution)/shard_map/reduce_scatter | solution.py:62
Sparse Core Ops, SparseCore 0:
  44.6 164.6 all-reduce.1
  212.2 44.6 reduce-scatter.1
Sparse Core Ops, SparseCore 1:
  48.6 84.8 all-gather.2
